TPU v7x, 32 devices: a whole 2x2x4 slice. The times are simulated.
32 devices in a mesh: grp: 2 (over x), seq: 8 (over z, y), mdl: 2 (over core).
Axes of the slice: x: 2, y: 2, z: 4, core: 2. Of those that a mesh axis runs over, the one named last changes fastest.
Arguments:
- signal: float32 [8, 128, 8192], P('grp', 'mdl', 'seq'), parts along dimension 0, may hold values from -6 to 6
- lengths: int32 [8], P('grp'), parts along dimension 0, may hold values from 1 to 64, 160 in all
- chan_weight: bfloat16 [128, 128, 16], P('mdl'), may hold values from -0.5 to 0.5
- up_weight: bfloat16 [4, 2048, 4096], P(None, 'seq', 'mdl'), may hold values from -0.125 to 0.125
- down_weight: bfloat16 [4, 2048, 4096], P(None, 'seq', 'mdl'), may hold values from -0.09375 to 0.09375
Outputs:
- features: bfloat16 [8, 64, 2048], P(('grp', 'mdl'), 'seq'), parts along dimension 0
There are 2 independent parts, one for each index of `grp`. A program takes and returns all parts, laid end to end along the dimension named above; an argument that names none is the same for every part. Nothing has to cross between parts.
Inputs may be any that keep to these rules, and one draw needn't show every extreme that they name: `lengths`: live windows of each recording; one recording is live for all 64, and all recordings together have (320) // 2.
All inputs are finite; a program needn't handle non-finite values.
Results may differ from a plain program's by a relative error of at most 0.014.
Values may be sent and summed in bfloat16 or wider, within the bound.
A program may use at most 128 MiB of HBM per device.

v0:
```python
import math
import jax
import jax.numpy as jnp
from jax import lax
from jax.sharding import PartitionSpec as P

HOP = 128
EPSILON = 1e-06


def shifted(x, axis, by):
    size = lax.axis_size(axis)
    pairs = [(i, i + by) for i in range(size) if 0 <= i + by < size]
    return lax.ppermute(x, axis, pairs)


def shifted_2(value, axis, steps):
    count = lax.axis_size(axis)
    pairs = [(source, (source + steps) % count) for source in range(count)]
    return lax.ppermute(value, axis, pairs)


def spectral_table(half_span):
    full_span = 2 * half_span
    row_index = jnp.arange(full_span, dtype=jnp.int32)
    col_index = jnp.arange(half_span, dtype=jnp.int32)
    phases = row_index[:, None] * col_index[None, :] % full_span
    angles = phases.astype(jnp.float32) * (2.0 * math.pi / full_span)
    window_taper = 0.5 - 0.5 * jnp.cos(row_index.astype(jnp.float32) * (2.0 * math.pi / full_span))
    weighting = window_taper * (1.0 / math.sqrt(full_span))
    joined = jnp.concatenate([jnp.cos(angles), -jnp.sin(angles)], axis=1) * weighting[:, None]
    return jnp.concatenate([joined[:half_span], joined[half_span:]], axis=1)


def log_power(spectrum):
    half_span = spectrum.shape[-1] // 2
    real_part = spectrum[..., :half_span]
    imag_part = spectrum[..., half_span:]
    return jnp.log1p(real_part * real_part + imag_part * imag_part).astype(jnp.bfloat16)


def normalize(state_rows):
    values = state_rows.astype(jnp.float32)
    scaled = values * lax.rsqrt(jnp.mean(values * values, axis=1, keepdims=True) + EPSILON)
    return (values, scaled.astype(jnp.bfloat16))


def project_down(hidden, own_down):
    return lax.dot_general(
        hidden, own_down, (((1,), (1,)), ((), ())), preferred_element_type=jnp.float32
    )


def apply_layer(state_rows, own_up, own_down):
    values, normed = normalize(state_rows)
    hidden = jax.nn.gelu(jnp.dot(normed, own_up, preferred_element_type=jnp.float32)).astype(
        jnp.bfloat16
    )
    summed = lax.psum(project_down(hidden, own_down), "mdl")
    return (values + summed).astype(jnp.bfloat16)


def body(signal, lengths, chan_weight, up_weight, down_weight):
    streams, channels, samples = signal.shape
    frames = samples // HOP
    dft_table = spectral_table(HOP)
    boundary = shifted(signal[:, :, :HOP], "seq", -1)
    local_part = jnp.dot(
        signal.reshape(streams, channels, frames, HOP), dft_table, precision=lax.Precision.HIGHEST
    )
    edge_part = jnp.dot(boundary, dft_table[:, 2 * HOP :], precision=lax.Precision.HIGHEST)
    following = jnp.concatenate([local_part[:, :, 1:, 2 * HOP :], edge_part[:, :, None, :]], axis=2)
    spectrum = local_part[..., : 2 * HOP] + following
    logpower = log_power(spectrum)
    embedded = jnp.einsum(
        "scfb,cbe->sfce", logpower, chan_weight, preferred_element_type=jnp.float32
    )
    embedded = embedded.reshape(streams, frames, channels * chan_weight.shape[2])
    frame_index = lax.axis_index("seq") * frames + jnp.arange(frames, dtype=jnp.int32)
    live_mask = frame_index[None, :] < lengths[:, None]
    tokens = jnp.where(live_mask[:, :, None], embedded, 0.0).astype(jnp.bfloat16)
    layer_count = up_weight.shape[0]
    group_size = lax.axis_size("seq") // layer_count
    own_up, own_down = (
        lax.all_to_all(
            jnp.repeat(up_weight, group_size, axis=0),
            "seq",
            split_axis=0,
            concat_axis=1,
            tiled=True,
        ),
        lax.all_to_all(
            jnp.repeat(down_weight, group_size, axis=0),
            "seq",
            split_axis=0,
            concat_axis=1,
            tiled=True,
        ),
    )
    own_up = own_up[0]
    own_down = own_down[0]
    layer_index = lax.axis_index("seq") // group_size
    state_rows = lax.all_gather(tokens, "mdl", axis=2, tiled=True)
    kept_shape = state_rows.shape
    state_rows = state_rows.reshape(kept_shape[0] * kept_shape[1], kept_shape[2])
    for turn_number in range(2 * layer_count):
        if turn_number < 2 * layer_count - 1:
            offset = turn_number - layer_index
            active = (offset >= 0) & (offset < layer_count)
            state_rows = jnp.where(active, apply_layer(state_rows, own_up, own_down), state_rows)
        state_rows = shifted_2(state_rows, "seq", group_size)
    full_rows = state_rows.reshape(kept_shape)
    half_streams = kept_shape[0] // lax.axis_size("mdl")
    return lax.dynamic_slice_in_dim(
        full_rows, lax.axis_index("mdl") * half_streams, half_streams, 0
    )


def solution(mesh):
    return jax.shard_map(
        body,
        mesh=mesh,
        in_specs=(
            P("grp", "mdl", "seq"),
            P("grp"),
            P("mdl", None, None),
            P(None, "seq", "mdl"),
            P(None, "seq", "mdl"),
        ),
        out_specs=P(("grp", "mdl"), "seq", None),
        check_vma=False,
    )
```

profile of v0, /device:TPU:0, one launch (start us, length us, event | category | flops | bytes accessed | tf_op | source)
XLA Modules:
  0.0 677.4 jit_solution(12882907544633261924)
XLA Ops:
  6.5 6.8 %broadcast_in_dim.22 = bf16[4,2,256,2048]{3,2,1,0:T(8,128)(2,1)} broadcast(bf16[4,256,2048]{2,1,0:T(8,128)(2,1)} %param.9), dimensions={0,2,3} | broadcast | bytes 12582912 | tf_op jit(solution)/shard_map/broadcast_in_dim | solution.py:93
  13.3 190.7 %all_to_all.8 = bf16[8,256,2048]{2,1,0:T(8,128)(2,1)} all-to-all(bf16[8,256,2048]{2,1,0:T(8,128)(2,1)} %bitcast.67), channel_id=1, replica_groups=mesh['grp'=2,'seq'=8,'mdl'=2] {'seq'}, dimensions={0} | all-to-all | bytes 16777216 | tf_op jit(solution)/shard_map/all_to_all | solution.py:92
  204.0 4.3 broadcast_in_dim.21
  208.3 5.2 all-to-all-start
  215.6 3.5 convolution_bitcast_fusion
  219.2 2.0 copy-done.1
  221.4 42.6 %collective-permute-done = f32[4,64,128]{2,1,0:T(8,128)S(1)} collective-permute-done((f32[4,64,128]{2,1,0:T(8,128)S(1)}, f32[4,64,128]{2,1,0:T(8,128)S(1)}, u32[]{:S(2)}, u32[]{:S(2)}) %collective-permute-start) | collective-permute-done | bytes 131104 | tf_op jit(solution)/shard_map/ppermute | solution.py:14
  264.4 1.9 slice_add_fusion
  270.3 126.8 %all-to-all-done = bf16[8,256,2048]{2,1,0:T(8,128)(2,1)} async-done(((bf16[8,256,2048]{2,1,0:T(8,128)(2,1)}), bf16[8,256,2048]{2,1,0:T(8,128)(2,1)}, u32[]{:S(2)}, u32[]{:S(2)}) %all-to-all-start) | async-done | bytes 8388640 | tf_op jit(solution)/shard_map/all_to_all | solution.py:85
  397.1 10.6 %fusion.143 = f32[32,2048]{1,0:T(8,128)} fusion(bf16[2048,2048]{1,0:T(8,128)(2,1)} %bitcast.59, bf16[2048,2048]{1,0:T(8,128)(2,1)} %bitcast.12, bf16[4,8,2048]{2,1,0:T(8,128)(2,1)S(1)} %all_gather.3, f32[4,8]{1,0:T(4,128)S(1)} %add_rsqrt_fusion), kind=kOutput, calls=%fused_computation.146 | convolution fusion | flops 537657344 | bytes 17170560 | tf_op jit(solution)/shard_map/dot_general | solution.py:49
  407.9 23.9 %all-reduce.8.cloned.1.call-done = f32[32,2048]{1,0:T(8,128)} async-done(((f32[32,2048]{1,0:T(8,128)}), f32[32,2048]{1,0:T(8,128)}) %all-reduce.8.cloned.1.call-update) | async-done | bytes 262160 | tf_op jit(solution)/shard_map/psum | solution.py:59
  434.6 5.8 collective-permute-done.1
  440.6 10.6 %fusion.135 = f32[32,2048]{1,0:T(8,128)} fusion(bf16[2048,2048]{1,0:T(8,128)(2,1)} %bitcast.60, bf16[2048,2048]{1,0:T(8,128)(2,1)} %bitcast.12, bf16[32,2048]{1,0:T(8,128)(2,1)S(1)} %collective-permute-done.1, f32[32]{0:T(128)S(1)} %add_rsqrt_fusion.6), kind=kOutput, calls=%fused_computation.144 | convolution fusion | flops 537657344 | bytes 17170560 | tf_op jit(solution)/shard_map/dot_general | solution.py:49
  451.2 17.7 %all-reduce.10.cloned.1.call-done = f32[32,2048]{1,0:T(8,128)} async-done(((f32[32,2048]{1,0:T(8,128)}), f32[32,2048]{1,0:T(8,128)}) %all-reduce.10.cloned.1.call-update) | async-done | bytes 262160 | tf_op jit(solution)/shard_map/psum | solution.py:59
  471.7 5.8 collective-permute-done.2
  477.7 10.6 %fusion.127 = f32[32,2048]{1,0:T(8,128)} fusion(bf16[2048,2048]{1,0:T(8,128)(2,1)} %bitcast.61, bf16[2048,2048]{1,0:T(8,128)(2,1)} %bitcast.12, bf16[32,2048]{1,0:T(8,128)(2,1)S(1)} %collective-permute-done.2, f32[32]{0:T(128)S(1)} %add_rsqrt_fusion.5), kind=kOutput, calls=%fused_computation.142 | convolution fusion | flops 537657344 | bytes 17170560 | tf_op jit(solution)/shard_map/dot_general | solution.py:49
  488.3 17.7 %all-reduce.12.cloned.1.call-done = f32[32,2048]{1,0:T(8,128)} async-done(((f32[32,2048]{1,0:T(8,128)}), f32[32,2048]{1,0:T(8,128)}) %all-reduce.12.cloned.1.call-update) | async-done | bytes 262160 | tf_op jit(solution)/shard_map/psum | solution.py:59
  508.8 5.8 collective-permute-done.3
  514.7 10.6 %fusion.119 = f32[32,2048]{1,0:T(8,128)} fusion(bf16[2048,2048]{1,0:T(8,128)(2,1)} %bitcast.62, bf16[2048,2048]{1,0:T(8,128)(2,1)} %bitcast.12, bf16[32,2048]{1,0:T(8,128)(2,1)S(1)} %collective-permute-done.3, f32[32]{0:T(128)S(1)} %add_rsqrt_fusion.4), kind=kOutput, calls=%fused_computation.140 | convolution fusion | flops 537657344 | bytes 17170560 | tf_op jit(solution)/shard_map/dot_general | solution.py:49
  525.4 17.7 %all-reduce.14.cloned.1.call-done = f32[32,2048]{1,0:T(8,128)} async-done(((f32[32,2048]{1,0:T(8,128)}), f32[32,2048]{1,0:T(8,128)}) %all-reduce.14.cloned.1.call-update) | async-done | bytes 262160 | tf_op jit(solution)/shard_map/psum | solution.py:59
  544.1 2.0 collective-permute-start.4
  546.1 5.8 collective-permute-done.4
  552.0 10.6 %fusion.111 = f32[32,2048]{1,0:T(8,128)} fusion(bf16[2048,2048]{1,0:T(8,128)(2,1)} %bitcast.63, bf16[2048,2048]{1,0:T(8,128)(2,1)} %bitcast.12, bf16[32,2048]{1,0:T(8,128)(2,1)S(1)} %collective-permute-done.4, f32[32]{0:T(128)S(1)} %add_rsqrt_fusion.3), kind=kOutput, calls=%fused_computation.138 | convolution fusion | flops 537657344 | bytes 17170560 | tf_op jit(solution)/shard_map/dot_general | solution.py:49
  562.7 17.7 %all-reduce.16.cloned.1.call-done = f32[32,2048]{1,0:T(8,128)} async-done(((f32[32,2048]{1,0:T(8,128)}), f32[32,2048]{1,0:T(8,128)}) %all-reduce.16.cloned.1.call-update) | async-done | bytes 262160 | tf_op jit(solution)/shard_map/psum | solution.py:59
  583.2 5.8 collective-permute-done.5
  589.1 10.6 %fusion.103 = f32[32,2048]{1,0:T(8,128)} fusion(bf16[2048,2048]{1,0:T(8,128)(2,1)} %bitcast.64, bf16[2048,2048]{1,0:T(8,128)(2,1)} %bitcast.12, bf16[32,2048]{1,0:T(8,128)(2,1)S(1)} %collective-permute-done.5, f32[32]{0:T(128)S(1)} %add_rsqrt_fusion.2), kind=kOutput, calls=%fused_computation.136 | convolution fusion | flops 537657344 | bytes 17170560 | tf_op jit(solution)/shard_map/dot_general | solution.py:49
  599.8 17.7 %all-reduce.18.cloned.1.call-done = f32[32,2048]{1,0:T(8,128)} async-done(((f32[32,2048]{1,0:T(8,128)}), f32[32,2048]{1,0:T(8,128)}) %all-reduce.18.cloned.1.call-update) | async-done | bytes 262160 | tf_op jit(solution)/shard_map/psum | solution.py:59
  620.3 5.8 collective-permute-done.6
  626.2 10.6 %fusion.95 = f32[32,2048]{1,0:T(8,128)} fusion(bf16[2048,2048]{1,0:T(8,128)(2,1)} %bitcast.65, bf16[2048,2048]{1,0:T(8,128)(2,1)} %bitcast.12, bf16[32,2048]{1,0:T(8,128)(2,1)S(1)} %collective-permute-done.6, f32[32]{0:T(128)S(1)} %add_rsqrt_fusion.1), kind=kOutput, calls=%fused_computation.134 | convolution fusion | flops 537657344 | bytes 17170560 | tf_op jit(solution)/shard_map/dot_general | solution.py:49
  636.8 17.7 %all-reduce.20.cloned.1.call-done = f32[32,2048]{1,0:T(8,128)} async-done(((f32[32,2048]{1,0:T(8,128)}), f32[32,2048]{1,0:T(8,128)}) %all-reduce.20.cloned.1.call-update) | async-done | bytes 262160 | tf_op jit(solution)/shard_map/psum | solution.py:59
  657.3 5.8 collective-permute-done.7
  663.1 6.8 collective-permute-done.8
  (68 shorter events, 26.4 us)
Async XLA Ops:
  6.5 260.2 %copy-start = (bf16[64,128,16]{1,2,0:T(8,128)(2,1)S(1)}, bf16[64,128,16]{1,2,0:T(8,128)(2,1)}, u32[]{:S(2)}) copy-start(bf16[64,128,16]{1,2,0:T(8,128)(2,1)} %param.7) | copy-start | bytes 786436
  13.3 190.7 %copy-start.2 = (bf16[4,256,2048]{2,1,0:T(8,128)(2,1)S(1)}, bf16[4,256,2048]{2,1,0:T(8,128)(2,1)}, u32[]{:S(2)}) copy-start(bf16[4,256,2048]{2,1,0:T(8,128)(2,1)} %param.8) | copy-start | bytes 12582916
  208.3 5.2 copy-start.3
  208.3 188.8 %all-to-all-start = ((bf16[8,256,2048]{2,1,0:T(8,128)(2,1)}), bf16[8,256,2048]{2,1,0:T(8,128)(2,1)}, u32[]{:S(2)}, u32[]{:S(2)}) async-start(bf16[8,256,2048]{2,1,0:T(8,128)(2,1)} %bitcast.66), calls=%async_computation | async-start | bytes 16777216 | tf_op jit(solution)/shard_map/all_to_all | solution.py:85
  213.5 7.9 %copy-start.4 = (s32[4]{0:T(128)S(1)}, s32[4]{0:T(128)}, u32[]{:S(2)}) copy-start(s32[4]{0:T(128)} %param.6) | copy-start | bytes 52
  213.5 218.4 %all-reduce.8.cloned.1.call-start = ((), (), s32[]{:S(2)}) async-start(), calls=%async_computation.2 | async-start | bytes 524288 | tf_op jit(solution)/shard_map/psum | solution.py:59
  213.6 50.4 %collective-permute-start = (f32[4,64,128]{2,1,0:T(8,128)S(1)}, f32[4,64,128]{2,1,0:T(8,128)S(1)}, u32[]{:S(2)}, u32[]{:S(2)}) collective-permute-start(f32[4,64,128]{2,1,0:T(8,128)S(1)} %slice.25), channel_id=1, source_target_pairs={{2,0},{4,2},{6,4},{8,6},{10,8},{12,10},{14,12},{3,1},{5,3},{7,5},{... | collective-permute-start | bytes 393224 | tf_op jit(solution)/shard_map/ppermute | solution.py:14
  219.2 2.0 copy-start.1
  407.7 61.3 %all-reduce.10.cloned.1.call-start = ((), (), s32[]{:S(2)}) async-start(), calls=%async_computation.3 | async-start | bytes 524288 | tf_op jit(solution)/shard_map/psum | solution.py:59
  432.8 7.6 %collective-permute-start.1 = (bf16[32,2048]{1,0:T(8,128)(2,1)S(1)}, bf16[32,2048]{1,0:T(8,128)(2,1)S(1)}, u32[]{:S(2)}, u32[]{:S(2)}) collective-permute-start(bf16[32,2048]{1,0:T(8,128)(2,1)S(1)} %fusion.85), channel_id=1, source_target_pairs={{0,4},{2,6},{4,8},{6,10},{8,12},{10,14},{12,0},{14,2},{1,5},{3,7},... | collective-permute-start | bytes 393224 | tf_op jit(solution)/shard_map/ppermute | solution.py:20
  451.2 54.8 %all-reduce.12.cloned.1.call-start = ((), (), s32[]{:S(2)}) async-start(), calls=%async_computation.4 | async-start | bytes 524288 | tf_op jit(solution)/shard_map/psum | solution.py:59
  469.9 7.6 %collective-permute-start.2 = (bf16[32,2048]{1,0:T(8,128)(2,1)S(1)}, bf16[32,2048]{1,0:T(8,128)(2,1)S(1)}, u32[]{:S(2)}, u32[]{:S(2)}) collective-permute-start(bf16[32,2048]{1,0:T(8,128)(2,1)S(1)} %fusion.91), channel_id=1, source_target_pairs={{0,4},{2,6},{4,8},{6,10},{8,12},{10,14},{12,0},{14,2},{1,5},{3,7},... | collective-permute-start | bytes 393224 | tf_op jit(solution)/shard_map/ppermute | solution.py:20
  488.3 54.8 %all-reduce.14.cloned.1.call-start = ((), (), s32[]{:S(2)}) async-start(), calls=%async_computation.5 | async-start | bytes 524288 | tf_op jit(solution)/shard_map/psum | solution.py:59
  507.0 7.6 %collective-permute-start.3 = (bf16[32,2048]{1,0:T(8,128)(2,1)S(1)}, bf16[32,2048]{1,0:T(8,128)(2,1)S(1)}, u32[]{:S(2)}, u32[]{:S(2)}) collective-permute-start(bf16[32,2048]{1,0:T(8,128)(2,1)S(1)} %fusion.90), channel_id=1, source_target_pairs={{0,4},{2,6},{4,8},{6,10},{8,12},{10,14},{12,0},{14,2},{1,5},{3,7},... | collective-permute-start | bytes 393224 | tf_op jit(solution)/shard_map/ppermute | solution.py:20
  525.4 55.0 %all-reduce.16.cloned.1.call-start = ((), (), s32[]{:S(2)}) async-start(), calls=%async_computation.6 | async-start | bytes 524288 | tf_op jit(solution)/shard_map/psum | solution.py:59
  544.1 7.8 %collective-permute-start.4 = (bf16[32,2048]{1,0:T(8,128)(2,1)S(1)}, bf16[32,2048]{1,0:T(8,128)(2,1)S(1)}, u32[]{:S(2)}, u32[]{:S(2)}) collective-permute-start(bf16[32,2048]{1,0:T(8,128)(2,1)S(1)} %fusion.89), channel_id=1, source_target_pairs={{0,4},{2,6},{4,8},{6,10},{8,12},{10,14},{12,0},{14,2},{1,5},{3,7},... | collective-permute-start | bytes 393224 | tf_op jit(solution)/shard_map/ppermute | solution.py:20
  562.7 54.8 %all-reduce.18.cloned.1.call-start = ((), (), s32[]{:S(2)}) async-start(), calls=%async_computation.7 | async-start | bytes 524288 | tf_op jit(solution)/shard_map/psum | solution.py:59
  581.4 7.6 %collective-permute-start.5 = (bf16[32,2048]{1,0:T(8,128)(2,1)S(1)}, bf16[32,2048]{1,0:T(8,128)(2,1)S(1)}, u32[]{:S(2)}, u32[]{:S(2)}) collective-permute-start(bf16[32,2048]{1,0:T(8,128)(2,1)S(1)} %fusion.88), channel_id=1, source_target_pairs={{0,4},{2,6},{4,8},{6,10},{8,12},{10,14},{12,0},{14,2},{1,5},{3,7},... | collective-permute-start | bytes 393224 | tf_op jit(solution)/shard_map/ppermute | solution.py:20
  599.7 54.8 %all-reduce.20.cloned.1.call-start = ((), (), s32[]{:S(2)}) async-start(), calls=%async_computation.8 | async-start | bytes 524288 | tf_op jit(solution)/shard_map/psum | solution.py:59
  618.5 7.6 %collective-permute-start.6 = (bf16[32,2048]{1,0:T(8,128)(2,1)S(1)}, bf16[32,2048]{1,0:T(8,128)(2,1)S(1)}, u32[]{:S(2)}, u32[]{:S(2)}) collective-permute-start(bf16[32,2048]{1,0:T(8,128)(2,1)S(1)} %fusion.87), channel_id=1, source_target_pairs={{0,4},{2,6},{4,8},{6,10},{8,12},{10,14},{12,0},{14,2},{1,5},{3,7},... | collective-permute-start | bytes 393224 | tf_op jit(solution)/shard_map/ppermute | solution.py:20
  655.5 7.6 %collective-permute-start.7 = (bf16[32,2048]{1,0:T(8,128)(2,1)S(1)}, bf16[32,2048]{1,0:T(8,128)(2,1)S(1)}, u32[]{:S(2)}, u32[]{:S(2)}) collective-permute-start(bf16[32,2048]{1,0:T(8,128)(2,1)S(1)} %fusion.86), channel_id=1, source_target_pairs={{0,4},{2,6},{4,8},{6,10},{8,12},{10,14},{12,0},{14,2},{1,5},{3,7},... | collective-permute-start | bytes 393224 | tf_op jit(solution)/shard_map/ppermute | solution.py:20
  663.1 6.8 collective-permute-start.8
Sparse Core Ops, SparseCore 0:
  407.8 24.0 all-reduce.7
  451.3 17.5 all-reduce.9
  488.4 17.5 all-reduce.11
  525.5 17.5 all-reduce.13
  562.8 17.5 all-reduce.15
  599.9 17.5 all-reduce.17
  636.9 17.5 all-reduce.19
where the time goes:
time: 678 us; the launch traced here: 677 us
  waiting for transfers between devices  347 us (51%)
  blocking collectives  193 us (28%)
  matrix products  78.4 us (12%)
  starting transfers between devices  19.7 us (3%)
  local copies, waits for them, and re-layouts  14.9 us (2%)
  between operations  13.8 us (2%)
  other arithmetic  11.1 us (2%)
    all_to_all x1, blocking collectives, body(): lax.all_to_all(jnp.repeat(down_weight, group_size, axis=0), 'seq', split_...  191 us
    psum x7, waiting for transfers between devices, apply_layer(): summed = lax.psum(project_down(hidden, own_down), 'mdl')  130 us
    all_to_all x1, waiting for transfers between devices, body(): lax.all_to_all(jnp.repeat(up_weight, group_size, axis=0), 'seq', split_ax...  127 us
    dot_general x7, matrix products, project_down(): lax.dot_general(hidden, own_down, (((1,), (1,)), ((), ())), preferred_ele...  74.1 us
    ppermute x8, waiting for transfers between devices, shifted_2(): return lax.ppermute(value, axis, pairs)  47.4 us
    ppermute x1, waiting for transfers between devices, shifted(): return lax.ppermute(x, axis, pairs)  42.6 us
  transfers between devices with their start and end apart: 17, of which 17 were waited for; matrix products, arithmetic and copies ran while one was open for 1% of the time, Pallas kernels for 0%

commit v1 on v0

--- a/solution.py
+++ b/solution.py
@@ -56,7 +56,7 @@
     hidden = jax.nn.gelu(jnp.dot(normed, own_up, preferred_element_type=jnp.float32)).astype(
         jnp.bfloat16
     )
-    summed = lax.psum(project_down(hidden, own_down), "mdl")
+    summed = jnp.sum(lax.all_gather(project_down(hidden, own_down), "mdl"), axis=0)
     return (values + summed).astype(jnp.bfloat16)
 
 

time: 678 us -> 539 us (0.79)
  waiting for transfers between devices: 347 us -> 225 us
  blocking collectives: 193 us -> 208 us
  between operations: 13.8 us -> 0.35 us
  starting transfers between devices: 19.7 us -> 10.6 us
    psum x7 -> x0, waiting for transfers between devices: 130 us -> none  [apply_layer(): summed = lax.psum(project_down(hidden, own_down), 'mdl')]
    all_gather x0 -> x7, blocking collectives: none -> 15.5 us  [apply_layer(): lax.all_gather(project_down(hidden, own_down), 'mdl')]
    ppermute x8, starting transfers between devices: 12.8 us -> 4.12 us  [shifted_2(): return lax.ppermute(value, axis, pairs)]
    ppermute x8, waiting for transfers between devices: 47.4 us -> 56 us  [shifted_2(): return lax.ppermute(value, axis, pairs)]
  transfers between devices with their start and end apart: 17 -> 10, of which waited for: 17 -> 10; matrix products, arithmetic and copies ran while one was open for 1% -> 2% of each run, Pallas kernels for 0% -> 0%
where the time goes in v1:
time: 539 us; the launch traced here: 537 us
  waiting for transfers between devices  225 us (42%)
  blocking collectives  208 us (39%)
  matrix products  73.4 us (14%)
  local copies, waits for them, and re-layouts  14.9 us (3%)
  starting transfers between devices  10.6 us (2%)
    all_to_all x1, blocking collectives, body(): lax.all_to_all(jnp.repeat(down_weight, group_size, axis=0), 'seq', split_...  191 us
    all_to_all x1, waiting for transfers between devices, body(): lax.all_to_all(jnp.repeat(up_weight, group_size, axis=0), 'seq', split_ax...  127 us
    dot_general x7, matrix products, project_down(): lax.dot_general(hidden, own_down, (((1,), (1,)), ((), ())), preferred_ele...  69.1 us
    ppermute x8, waiting for transfers between devices, shifted_2(): return lax.ppermute(value, axis, pairs)  56 us
    ppermute x1, waiting for transfers between devices, shifted(): return lax.ppermute(x, axis, pairs)  42.6 us
    all_gather x7, blocking collectives, apply_layer(): lax.all_gather(project_down(hidden, own_down), 'mdl')  15.5 us
  transfers between devices with their start and end apart: 10, of which 10 were waited for; matrix products, arithmetic and copies ran while one was open for 2% of the time, Pallas kernels for 0%

profile of v1, /device:TPU:0, one launch (start us, length us, event | category | flops | bytes accessed | tf_op | source)
XLA Modules:
  0.0 537.4 jit_solution(3900778185091365195)
XLA Ops:
  0.0 6.8 %broadcast_in_dim.22 = bf16[4,2,256,2048]{3,2,1,0:T(8,128)(2,1)} broadcast(bf16[4,256,2048]{2,1,0:T(8,128)(2,1)} %param.9), dimensions={0,2,3} | broadcast | bytes 12582912 | tf_op jit(solution)/shard_map/broadcast_in_dim | solution.py:93
  6.8 190.7 %all_to_all.8 = bf16[8,256,2048]{2,1,0:T(8,128)(2,1)} all-to-all(bf16[8,256,2048]{2,1,0:T(8,128)(2,1)} %bitcast.74), channel_id=1, replica_groups=mesh['grp'=2,'seq'=8,'mdl'=2] {'seq'}, dimensions={0} | all-to-all | bytes 16777216 | tf_op jit(solution)/shard_map/all_to_all | solution.py:92
  197.5 4.3 broadcast_in_dim.21
  201.8 5.2 all-to-all-start
  209.0 3.5 convolution_bitcast_fusion
  212.6 2.0 copy-done.1
  214.9 42.6 %collective-permute-done = f32[4,64,128]{2,1,0:T(8,128)S(1)} collective-permute-done((f32[4,64,128]{2,1,0:T(8,128)S(1)}, f32[4,64,128]{2,1,0:T(8,128)S(1)}, u32[]{:S(2)}, u32[]{:S(2)}) %collective-permute-start) | collective-permute-done | bytes 131104 | tf_op jit(solution)/shard_map/ppermute | solution.py:14
  257.9 1.9 slice_add_fusion
  263.7 126.8 %all-to-all-done = bf16[8,256,2048]{2,1,0:T(8,128)(2,1)} async-done(((bf16[8,256,2048]{2,1,0:T(8,128)(2,1)}), bf16[8,256,2048]{2,1,0:T(8,128)(2,1)}, u32[]{:S(2)}, u32[]{:S(2)}) %all-to-all-start) | async-done | bytes 8388640 | tf_op jit(solution)/shard_map/all_to_all | solution.py:85
  390.5 9.9 %fusion.143 = f32[32,2048]{1,0:T(8,128)S(1)} fusion(bf16[2048,2048]{1,0:T(8,128)(2,1)} %bitcast.66, bf16[2048,2048]{1,0:T(8,128)(2,1)} %bitcast.12, bf16[4,8,2048]{2,1,0:T(8,128)(2,1)S(1)} %all_gather.45, f32[4,8]{1,0:T(4,128)S(1)} %add_rsqrt_fusion), kind=kOutput, calls=%fused_computation.146 | convolution fusion | flops 537657344 | bytes 17170560 | tf_op jit(solution)/shard_map/dot_general | solution.py:49
  400.4 2.4 all-gather
  402.9 7.3 %collective-permute-done.1 = bf16[32,2048]{1,0:T(8,128)(2,1)S(1)} collective-permute-done((bf16[32,2048]{1,0:T(8,128)(2,1)S(1)}, bf16[32,2048]{1,0:T(8,128)(2,1)S(1)}, u32[]{:S(2)}, u32[]{:S(2)}) %collective-permute-start.1) | collective-permute-done | bytes 131104 | tf_op jit(solution)/shard_map/ppermute | solution.py:20
  410.4 9.9 %fusion.135 = f32[32,2048]{1,0:T(8,128)S(1)} fusion(bf16[2048,2048]{1,0:T(8,128)(2,1)} %bitcast.67, bf16[2048,2048]{1,0:T(8,128)(2,1)} %bitcast.12, bf16[32,2048]{1,0:T(8,128)(2,1)S(1)} %collective-permute-done.1, f32[32]{0:T(128)S(1)} %add_rsqrt_fusion.6), kind=kOutput, calls=%fused_computation.144 | convolution fusion | flops 537657344 | bytes 17170560 | tf_op jit(solution)/shard_map/dot_general | solution.py:49
  420.2 2.2 all-gather.1
  422.5 3.4 collective-permute-start.2
  425.9 5.4 %collective-permute-done.2 = bf16[32,2048]{1,0:T(8,128)(2,1)S(1)} collective-permute-done((bf16[32,2048]{1,0:T(8,128)(2,1)S(1)}, bf16[32,2048]{1,0:T(8,128)(2,1)S(1)}, u32[]{:S(2)}, u32[]{:S(2)}) %collective-permute-start.2) | collective-permute-done | bytes 131104 | tf_op jit(solution)/shard_map/ppermute | solution.py:20
  431.5 9.9 %fusion.127 = f32[32,2048]{1,0:T(8,128)S(1)} fusion(bf16[2048,2048]{1,0:T(8,128)(2,1)} %bitcast.68, bf16[2048,2048]{1,0:T(8,128)(2,1)} %bitcast.12, bf16[32,2048]{1,0:T(8,128)(2,1)S(1)} %collective-permute-done.2, f32[32]{0:T(128)S(1)} %add_rsqrt_fusion.5), kind=kOutput, calls=%fused_computation.142 | convolution fusion | flops 537657344 | bytes 17170560 | tf_op jit(solution)/shard_map/dot_general | solution.py:49
  441.4 2.2 all-gather.2
  443.8 7.2 %collective-permute-done.3 = bf16[32,2048]{1,0:T(8,128)(2,1)S(1)} collective-permute-done((bf16[32,2048]{1,0:T(8,128)(2,1)S(1)}, bf16[32,2048]{1,0:T(8,128)(2,1)S(1)}, u32[]{:S(2)}, u32[]{:S(2)}) %collective-permute-start.3) | collective-permute-done | bytes 131104 | tf_op jit(solution)/shard_map/ppermute | solution.py:20
  451.2 9.9 %fusion.119 = f32[32,2048]{1,0:T(8,128)S(1)} fusion(bf16[2048,2048]{1,0:T(8,128)(2,1)} %bitcast.69, bf16[2048,2048]{1,0:T(8,128)(2,1)} %bitcast.12, bf16[32,2048]{1,0:T(8,128)(2,1)S(1)} %collective-permute-done.3, f32[32]{0:T(128)S(1)} %add_rsqrt_fusion.4), kind=kOutput, calls=%fused_computation.140 | convolution fusion | flops 537657344 | bytes 17170560 | tf_op jit(solution)/shard_map/dot_general | solution.py:49
  461.1 2.2 all-gather.3
  463.6 7.3 %collective-permute-done.4 = bf16[32,2048]{1,0:T(8,128)(2,1)S(1)} collective-permute-done((bf16[32,2048]{1,0:T(8,128)(2,1)S(1)}, bf16[32,2048]{1,0:T(8,128)(2,1)S(1)}, u32[]{:S(2)}, u32[]{:S(2)}) %collective-permute-start.4) | collective-permute-done | bytes 131104 | tf_op jit(solution)/shard_map/ppermute | solution.py:20
  471.1 9.9 %fusion.111 = f32[32,2048]{1,0:T(8,128)S(1)} fusion(bf16[2048,2048]{1,0:T(8,128)(2,1)} %bitcast.70, bf16[2048,2048]{1,0:T(8,128)(2,1)} %bitcast.12, bf16[32,2048]{1,0:T(8,128)(2,1)S(1)} %collective-permute-done.4, f32[32]{0:T(128)S(1)} %add_rsqrt_fusion.3), kind=kOutput, calls=%fused_computation.138 | convolution fusion | flops 537657344 | bytes 17170560 | tf_op jit(solution)/shard_map/dot_general | solution.py:49
  481.0 2.2 all-gather.4
  483.3 7.3 %collective-permute-done.5 = bf16[32,2048]{1,0:T(8,128)(2,1)S(1)} collective-permute-done((bf16[32,2048]{1,0:T(8,128)(2,1)S(1)}, bf16[32,2048]{1,0:T(8,128)(2,1)S(1)}, u32[]{:S(2)}, u32[]{:S(2)}) %collective-permute-start.5) | collective-permute-done | bytes 131104 | tf_op jit(solution)/shard_map/ppermute | solution.py:20
  490.8 9.9 %fusion.103 = f32[32,2048]{1,0:T(8,128)S(1)} fusion(bf16[2048,2048]{1,0:T(8,128)(2,1)} %bitcast.71, bf16[2048,2048]{1,0:T(8,128)(2,1)} %bitcast.12, bf16[32,2048]{1,0:T(8,128)(2,1)S(1)} %collective-permute-done.5, f32[32]{0:T(128)S(1)} %add_rsqrt_fusion.2), kind=kOutput, calls=%fused_computation.136 | convolution fusion | flops 537657344 | bytes 17170560 | tf_op jit(solution)/shard_map/dot_general | solution.py:49
  500.6 2.2 all-gather.5
  503.0 7.3 %collective-permute-done.6 = bf16[32,2048]{1,0:T(8,128)(2,1)S(1)} collective-permute-done((bf16[32,2048]{1,0:T(8,128)(2,1)S(1)}, bf16[32,2048]{1,0:T(8,128)(2,1)S(1)}, u32[]{:S(2)}, u32[]{:S(2)}) %collective-permute-start.6) | collective-permute-done | bytes 131104 | tf_op jit(solution)/shard_map/ppermute | solution.py:20
  510.4 9.9 %fusion.95 = f32[32,2048]{1,0:T(8,128)S(1)} fusion(bf16[2048,2048]{1,0:T(8,128)(2,1)} %bitcast.72, bf16[2048,2048]{1,0:T(8,128)(2,1)} %bitcast.12, bf16[32,2048]{1,0:T(8,128)(2,1)S(1)} %collective-permute-done.6, f32[32]{0:T(128)S(1)} %add_rsqrt_fusion.1), kind=kOutput, calls=%fused_computation.134 | convolution fusion | flops 537657344 | bytes 17170560 | tf_op jit(solution)/shard_map/dot_general | solution.py:49
  520.3 2.2 all-gather.6
  522.6 7.3 %collective-permute-done.7 = bf16[32,2048]{1,0:T(8,128)(2,1)S(1)} collective-permute-done((bf16[32,2048]{1,0:T(8,128)(2,1)S(1)}, bf16[32,2048]{1,0:T(8,128)(2,1)S(1)}, u32[]{:S(2)}, u32[]{:S(2)}) %collective-permute-start.7) | collective-permute-done | bytes 131104 | tf_op jit(solution)/shard_map/ppermute | solution.py:20
  530.0 6.8 %collective-permute-done.8 = bf16[32,2048]{1,0:T(8,128)(2,1)S(1)} collective-permute-done((bf16[32,2048]{1,0:T(8,128)(2,1)S(1)}, bf16[32,2048]{1,0:T(8,128)(2,1)S(1)}, u32[]{:S(2)}, u32[]{:S(2)}) %collective-permute-start.8) | collective-permute-done | bytes 131104 | tf_op jit(solution)/shard_map/ppermute | solution.py:20
  (61 shorter events, 9.2 us)
Async XLA Ops:
  0.0 260.2 %copy-start = (bf16[64,128,16]{1,2,0:T(8,128)(2,1)S(1)}, bf16[64,128,16]{1,2,0:T(8,128)(2,1)}, u32[]{:S(2)}) copy-start(bf16[64,128,16]{1,2,0:T(8,128)(2,1)} %param.7) | copy-start | bytes 786436
  6.8 190.7 %copy-start.2 = (bf16[4,256,2048]{2,1,0:T(8,128)(2,1)S(1)}, bf16[4,256,2048]{2,1,0:T(8,128)(2,1)}, u32[]{:S(2)}) copy-start(bf16[4,256,2048]{2,1,0:T(8,128)(2,1)} %param.8) | copy-start | bytes 12582916
  201.8 5.2 copy-start.3
  201.8 188.8 %all-to-all-start = ((bf16[8,256,2048]{2,1,0:T(8,128)(2,1)}), bf16[8,256,2048]{2,1,0:T(8,128)(2,1)}, u32[]{:S(2)}, u32[]{:S(2)}) async-start(bf16[8,256,2048]{2,1,0:T(8,128)(2,1)} %bitcast.73), calls=%async_computation | async-start | bytes 16777216 | tf_op jit(solution)/shard_map/all_to_all | solution.py:85
  207.0 7.8 %copy-start.4 = (s32[4]{0:T(128)S(1)}, s32[4]{0:T(128)}, u32[]{:S(2)}) copy-start(s32[4]{0:T(128)} %param.6) | copy-start | bytes 52
  207.0 50.5 %collective-permute-start = (f32[4,64,128]{2,1,0:T(8,128)S(1)}, f32[4,64,128]{2,1,0:T(8,128)S(1)}, u32[]{:S(2)}, u32[]{:S(2)}) collective-permute-start(f32[4,64,128]{2,1,0:T(8,128)S(1)} %slice.25), channel_id=1, source_target_pairs={{2,0},{4,2},{6,4},{8,6},{10,8},{12,10},{14,12},{3,1},{5,3},{7,5},{... | collective-permute-start | bytes 393224 | tf_op jit(solution)/shard_map/ppermute | solution.py:14
  212.6 2.0 copy-start.1
  402.8 7.4 %collective-permute-start.1 = (bf16[32,2048]{1,0:T(8,128)(2,1)S(1)}, bf16[32,2048]{1,0:T(8,128)(2,1)S(1)}, u32[]{:S(2)}, u32[]{:S(2)}) collective-permute-start(bf16[32,2048]{1,0:T(8,128)(2,1)S(1)} %fusion.85), channel_id=1, source_target_pairs={{0,4},{2,6},{4,8},{6,10},{8,12},{10,14},{12,0},{14,2},{1,5},{3,7},... | collective-permute-start | bytes 393224 | tf_op jit(solution)/shard_map/ppermute | solution.py:20
  422.5 8.9 %collective-permute-start.2 = (bf16[32,2048]{1,0:T(8,128)(2,1)S(1)}, bf16[32,2048]{1,0:T(8,128)(2,1)S(1)}, u32[]{:S(2)}, u32[]{:S(2)}) collective-permute-start(bf16[32,2048]{1,0:T(8,128)(2,1)S(1)} %fusion.91), channel_id=1, source_target_pairs={{0,4},{2,6},{4,8},{6,10},{8,12},{10,14},{12,0},{14,2},{1,5},{3,7},... | collective-permute-start | bytes 393224 | tf_op jit(solution)/shard_map/ppermute | solution.py:20
  443.7 7.4 %collective-permute-start.3 = (bf16[32,2048]{1,0:T(8,128)(2,1)S(1)}, bf16[32,2048]{1,0:T(8,128)(2,1)S(1)}, u32[]{:S(2)}, u32[]{:S(2)}) collective-permute-start(bf16[32,2048]{1,0:T(8,128)(2,1)S(1)} %fusion.90), channel_id=1, source_target_pairs={{0,4},{2,6},{4,8},{6,10},{8,12},{10,14},{12,0},{14,2},{1,5},{3,7},... | collective-permute-start | bytes 393224 | tf_op jit(solution)/shard_map/ppermute | solution.py:20
  463.3 7.6 %collective-permute-start.4 = (bf16[32,2048]{1,0:T(8,128)(2,1)S(1)}, bf16[32,2048]{1,0:T(8,128)(2,1)S(1)}, u32[]{:S(2)}, u32[]{:S(2)}) collective-permute-start(bf16[32,2048]{1,0:T(8,128)(2,1)S(1)} %fusion.89), channel_id=1, source_target_pairs={{0,4},{2,6},{4,8},{6,10},{8,12},{10,14},{12,0},{14,2},{1,5},{3,7},... | collective-permute-start | bytes 393224 | tf_op jit(solution)/shard_map/ppermute | solution.py:20
  483.2 7.4 %collective-permute-start.5 = (bf16[32,2048]{1,0:T(8,128)(2,1)S(1)}, bf16[32,2048]{1,0:T(8,128)(2,1)S(1)}, u32[]{:S(2)}, u32[]{:S(2)}) collective-permute-start(bf16[32,2048]{1,0:T(8,128)(2,1)S(1)} %fusion.88), channel_id=1, source_target_pairs={{0,4},{2,6},{4,8},{6,10},{8,12},{10,14},{12,0},{14,2},{1,5},{3,7},... | collective-permute-start | bytes 393224 | tf_op jit(solution)/shard_map/ppermute | solution.py:20
  502.9 7.4 %collective-permute-start.6 = (bf16[32,2048]{1,0:T(8,128)(2,1)S(1)}, bf16[32,2048]{1,0:T(8,128)(2,1)S(1)}, u32[]{:S(2)}, u32[]{:S(2)}) collective-permute-start(bf16[32,2048]{1,0:T(8,128)(2,1)S(1)} %fusion.87), channel_id=1, source_target_pairs={{0,4},{2,6},{4,8},{6,10},{8,12},{10,14},{12,0},{14,2},{1,5},{3,7},... | collective-permute-start | bytes 393224 | tf_op jit(solution)/shard_map/ppermute | solution.py:20
  522.6 7.4 %collective-permute-start.7 = (bf16[32,2048]{1,0:T(8,128)(2,1)S(1)}, bf16[32,2048]{1,0:T(8,128)(2,1)S(1)}, u32[]{:S(2)}, u32[]{:S(2)}) collective-permute-start(bf16[32,2048]{1,0:T(8,128)(2,1)S(1)} %fusion.86), channel_id=1, source_target_pairs={{0,4},{2,6},{4,8},{6,10},{8,12},{10,14},{12,0},{14,2},{1,5},{3,7},... | collective-permute-start | bytes 393224 | tf_op jit(solution)/shard_map/ppermute | solution.py:20
  530.0 6.8 %collective-permute-start.8 = (bf16[32,2048]{1,0:T(8,128)(2,1)S(1)}, bf16[32,2048]{1,0:T(8,128)(2,1)S(1)}, u32[]{:S(2)}, u32[]{:S(2)}) collective-permute-start(bf16[32,2048]{1,0:T(8,128)(2,1)S(1)} %collective-permute-done.7), channel_id=1, source_target_pairs={{0,4},{2,6},{4,8},{6,10},{8,12},{10,14},{12,0},{14,2},{1,5},{3,7},... | collective-permute-start | bytes 393224 | tf_op jit(solution)/shard_map/ppermute | solution.py:20
